TPU v7x, 128 devices: a whole 4x4x4 slice. The times are simulated.
128 devices in a mesh: freq: 8 (over y_hi, z), src: 16 (over y_lo, x, core).
Axes of the slice: x: 4, y: 4 (y_hi: 2, y_lo: 2; y = y_hi * 2 + y_lo), z: 4, core: 2. Of those that a mesh axis runs over, the one named last changes fastest.
Arguments:
- reflection: bfloat16 [2, 128, 2048, 2048], P(None, 'freq', None, 'src'), may hold values from -0.125 to 0.125
- direct_wave: float32 [2048, 128, 128], P('src', 'freq'), may hold values from -6 to 6
- first_arrival: int32 [2048, 64], P(('src', 'freq')), may hold values from 64 to 191
Outputs:
- focus_minus: float32 [2048, 128, 128], P('src', 'freq')
- focus_plus: float32 [2048, 128, 128], P('src', 'freq')
All inputs are finite; a program needn't handle non-finite values.
Results may differ from a plain program's by a relative error of at most 0.035.
Values may be sent and summed in bfloat16 or wider, within the bound.
A program may use at most 128 MiB of HBM per device.

v0:
```python
import math
import jax
import jax.numpy as jnp
from jax import lax
from jax.sharding import PartitionSpec as P

NT = 512
ITERS = 2


def transform_tables(nfreq, ntime):
    freqs = jnp.arange(1, nfreq + 1, dtype=jnp.int32)
    times = jnp.arange(ntime, dtype=jnp.int32)
    phase = (freqs[:, None] * times[None, :] % ntime).astype(jnp.float32) * (2.0 * math.pi / ntime)
    cosine = jnp.cos(phase)
    sine = jnp.sin(phase)
    inverse = jnp.stack([cosine * (2.0 / ntime), -sine * (2.0 / ntime)]).astype(jnp.bfloat16)
    forward = jnp.stack([cosine, -sine]).astype(jnp.bfloat16)
    return (inverse, forward)


def apply_window(spectrum, first_arrival, inverse, forward):
    rows_count, nfreq, width = spectrum.shape
    half = width // 2
    ntime = inverse.shape[2]
    split = spectrum.reshape(rows_count, nfreq, 2, half)
    signal = jnp.einsum("rfpc,pft->rct", split, inverse, preferred_element_type=jnp.float32)
    times = jnp.arange(ntime, dtype=jnp.int32)
    limit = first_arrival[:, :, None]
    keep = (times[None, None, :] < limit) | (times[None, None, :] > ntime - limit)
    windowed = jnp.where(keep, signal, jnp.zeros_like(signal)).astype(jnp.bfloat16)
    back = jnp.einsum("rct,pft->rfpc", windowed, forward, preferred_element_type=jnp.float32)
    return back.reshape(rows_count, nfreq, width)


def stacked_parts(vectors, factor):
    rounded = vectors.astype(jnp.bfloat16)
    half = rounded.shape[-1] // 2
    swapped = jnp.concatenate([-rounded[..., half:], rounded[..., :half]], axis=-1)
    if factor < 0:
        swapped = -swapped
    return jnp.stack([rounded, swapped])


def to_owners(reflection, vectors, factor):
    operand = stacked_parts(vectors, factor)
    summed = lax.psum_scatter(
        jnp.einsum(
            "pfrs,psfk->rfk", reflection, operand, preferred_element_type=jnp.float32
        ).astype(jnp.bfloat16),
        "src",
        scatter_dimension=0,
        tiled=True,
    )
    return lax.all_to_all(summed, "freq", split_axis=0, concat_axis=1, tiled=True)


def to_groups(spectrum):
    return lax.all_to_all(
        spectrum.astype(jnp.bfloat16), "freq", split_axis=1, concat_axis=0, tiled=True
    ).astype(spectrum.dtype)


def local(reflection, direct_wave, first_arrival):
    nfreq = direct_wave.shape[1] * lax.axis_size("freq")
    inverse, forward = transform_tables(nfreq, NT)
    focus_plus = direct_wave
    focus_minus = direct_wave
    for iteration in range(ITERS):
        spectrum = to_owners(reflection, focus_plus, 1.0)
        focus_minus = to_groups(apply_window(spectrum, first_arrival, inverse, forward))
        spectrum = to_owners(reflection, focus_minus, -1.0)
        update = to_groups(apply_window(spectrum, first_arrival, inverse, forward))
        focus_plus = direct_wave + update
    return (focus_minus, focus_plus)


def solution(mesh):
    in_specs = (P(None, "freq", None, "src"), P("src", "freq", None), P(("src", "freq"), None))
    out_specs = (P("src", "freq", None), P("src", "freq", None))
    return jax.shard_map(local, mesh=mesh, in_specs=in_specs, out_specs=out_specs, check_vma=False)
```

profile of v0, /device:TPU:0, one launch (start us, length us, event | category | flops | bytes accessed | tf_op | source)
XLA Modules:
  0.0 548.1 jit_solution(8581948061272657369)
XLA Ops:
  7.2 1.6 copy.115
  9.1 11.0 %bitcast_convert_fusion.3 = bf16[16,128,2048]{2,1,0:T(8,128)(2,1)} fusion(bf16[2,16,2048,128]{3,2,1,0:T(8,128)(2,1)} %param.3, bf16[1,128,16,128]{1,3,0,2:T(8,128)(2,1)S(1)} %maximum_bitcast_fusion, bf16[1,128,16,128]{1,3,0,2:T(8,128)(2,1)S(1)} %convert_bitcast_fusion.2), kind=kOutput, calls=%fused_computation.3 | convolution fusion | flops 2152202240 | bytes 26214400 | tf_op jit(solution)/shard_map/pfrs,psfk->rfk/dot_general | solution.py:48
  20.1 12.3 %copy.159 = bf16[2048,2048]{1,0:T(8,128)(2,1)} copy(bf16[2048,2048]{0,1:T(8,128)(2,1)} %bitcast.177) | data formatting | bytes 16777216
  32.4 77.2 %reduce-scatter.13.cloned.1.call-done = bf16[128,2048]{1,0:T(8,128)(2,1)} async-done(((bf16[2048,2048]{1,0:T(8,128)(2,1)}), bf16[128,2048]{1,0:T(8,128)(2,1)}) %reduce-scatter.13.cloned.1.call-update) | async-done | bytes 524304
  109.6 1.3 copy.160
  110.9 1.2 copy.96
  112.1 6.6 %all-to-all-start = ((bf16[128,16,128]{2,1,0:T(8,128)(2,1)}), bf16[128,16,128]{2,1,0:T(8,128)(2,1)S(1)}, u32[]{:S(2)}, u32[]{:S(2)}) async-start(bf16[128,16,128]{2,1,0:T(8,128)(2,1)} %copy.96), calls=%async_computation | async-start | bytes 1048576 | tf_op jit(solution)/shard_map/all_to_all | solution.py:55
  118.8 1.9 fusion.69
  120.7 7.8 %all-to-all-done = bf16[128,16,128]{2,1,0:T(8,128)(2,1)S(1)} async-done(((bf16[128,16,128]{2,1,0:T(8,128)(2,1)}), bf16[128,16,128]{2,1,0:T(8,128)(2,1)S(1)}, u32[]{:S(2)}, u32[]{:S(2)}) %all-to-all-start) | async-done | bytes 524320 | tf_op jit(solution)/shard_map/all_to_all | solution.py:55
  129.0 1.8 fusion.25
  131.3 13.1 %all_to_all.114 = bf16[16,128,128]{2,0,1:T(8,128)(2,1)S(1)} all-to-all(bf16[16,128,128]{2,0,1:T(8,128)(2,1)S(1)} %copy.100), channel_id=1, replica_groups=mesh['freq'=8,'src'=16] {'freq'}, dimensions={1} | all-to-all | bytes 1048576 | tf_op jit(solution)/shard_map/all_to_all | solution.py:59
  144.5 0.5 copy.106
  145.2 0.5 copy.167
  145.7 0.5 copy.168
  146.3 11.0 %bitcast_convert_fusion.2 = bf16[16,128,2048]{2,1,0:T(8,128)(2,1)} fusion(bf16[2,16,2048,128]{3,2,1,0:T(8,128)(2,1)} %param.3, bf16[1,128,16,128]{1,3,0,2:T(8,128)(2,1)S(1)} %maximum_negate_fusion, bf16[1,128,16,128]{1,3,0,2:T(8,128)(2,1)S(1)} %copy.106), kind=kOutput, calls=%fused_computation.2 | convolution fusion | flops 2152202240 | bytes 26214400 | tf_op jit(solution)/shard_map/pfrs,psfk->rfk/dot_general | solution.py:48
  157.3 12.3 %copy.161 = bf16[2048,2048]{1,0:T(8,128)(2,1)} copy(bf16[2048,2048]{0,1:T(8,128)(2,1)} %bitcast.178) | data formatting | bytes 16777216
  169.7 71.8 %reduce-scatter.15.cloned.1.call-done = bf16[128,2048]{1,0:T(8,128)(2,1)} async-done(((bf16[2048,2048]{1,0:T(8,128)(2,1)}), bf16[128,2048]{1,0:T(8,128)(2,1)}) %reduce-scatter.15.cloned.1.call-update) | async-done | bytes 524304
  241.4 1.3 copy.162
  242.7 0.4 copy.108
  243.2 16.5 %all_to_all.115 = bf16[128,16,128]{2,1,0:T(8,128)(2,1)S(1)} all-to-all(bf16[128,16,128]{2,1,0:T(8,128)(2,1)S(1)} %copy.108), channel_id=1, replica_groups=mesh['freq'=8,'src'=16] {'freq'}, dimensions={0} | all-to-all | bytes 1048576 | tf_op jit(solution)/shard_map/all_to_all | solution.py:55
  260.1 1.8 fusion.26
  262.4 12.7 %all_to_all.116 = bf16[16,128,128]{2,0,1:T(8,128)(2,1)S(1)} all-to-all(bf16[16,128,128]{2,0,1:T(8,128)(2,1)S(1)} %copy.112), channel_id=1, replica_groups=mesh['freq'=8,'src'=16] {'freq'}, dimensions={1} | all-to-all | bytes 1048576 | tf_op jit(solution)/shard_map/all_to_all | solution.py:59
  275.4 1.1 copy.114
  276.5 1.6 copy.116
  278.3 11.0 %bitcast_convert_fusion.1 = bf16[16,128,2048]{2,1,0:T(8,128)(2,1)} fusion(bf16[2,16,2048,128]{3,2,1,0:T(8,128)(2,1)} %param.3, bf16[1,128,16,128]{1,3,0,2:T(8,128)(2,1)S(1)} %maximum_bitcast_fusion.1, bf16[1,128,16,128]{1,3,0,2:T(8,128)(2,1)S(1)} %bitcast.185), kind=kOutput, calls=%fused_computation.1 | convolution fusion | flops 2152202240 | bytes 26214400 | tf_op jit(solution)/shard_map/pfrs,psfk->rfk/dot_general | solution.py:48
  289.3 12.3 %copy.163 = bf16[2048,2048]{1,0:T(8,128)(2,1)} copy(bf16[2048,2048]{0,1:T(8,128)(2,1)} %bitcast.179) | data formatting | bytes 16777216
  301.7 71.6 %reduce-scatter.17.cloned.1.call-done = bf16[128,2048]{1,0:T(8,128)(2,1)} async-done(((bf16[2048,2048]{1,0:T(8,128)(2,1)}), bf16[128,2048]{1,0:T(8,128)(2,1)}) %reduce-scatter.17.cloned.1.call-update) | async-done | bytes 524304
  373.3 1.3 copy.164
  374.6 0.4 copy.119
  375.1 16.6 %all_to_all.117 = bf16[128,16,128]{2,1,0:T(8,128)(2,1)S(1)} all-to-all(bf16[128,16,128]{2,1,0:T(8,128)(2,1)S(1)} %copy.119), channel_id=1, replica_groups=mesh['freq'=8,'src'=16] {'freq'}, dimensions={0} | all-to-all | bytes 1048576 | tf_op jit(solution)/shard_map/all_to_all | solution.py:55
  392.2 0.9 fusion.27
  393.6 12.7 %all_to_all.118 = bf16[16,128,128]{2,0,1:T(8,128)(2,1)S(1)} all-to-all(bf16[16,128,128]{2,0,1:T(8,128)(2,1)S(1)} %copy.123), channel_id=1, replica_groups=mesh['freq'=8,'src'=16] {'freq'}, dimensions={1} | all-to-all | bytes 1048576 | tf_op jit(solution)/shard_map/all_to_all | solution.py:59
  406.5 0.5 copy.129
  407.2 0.5 copy.169
  407.7 0.5 copy.170
  408.3 11.0 %bitcast_convert_fusion = bf16[16,128,2048]{2,1,0:T(8,128)(2,1)} fusion(bf16[2,16,2048,128]{3,2,1,0:T(8,128)(2,1)} %param.3, bf16[1,128,16,128]{1,3,0,2:T(8,128)(2,1)S(1)} %maximum_negate_fusion.1, bf16[1,128,16,128]{1,3,0,2:T(8,128)(2,1)S(1)} %copy.129), kind=kOutput, calls=%fused_computation | convolution fusion | flops 2152202240 | bytes 26214400 | tf_op jit(solution)/shard_map/pfrs,psfk->rfk/dot_general | solution.py:48
  419.3 12.3 %copy.165 = bf16[2048,2048]{1,0:T(8,128)(2,1)} copy(bf16[2048,2048]{0,1:T(8,128)(2,1)} %bitcast.180) | data formatting | bytes 16777216
  431.6 71.6 %reduce-scatter.19.cloned.1.call-done = bf16[128,2048]{1,0:T(8,128)(2,1)} async-done(((bf16[2048,2048]{1,0:T(8,128)(2,1)}), bf16[128,2048]{1,0:T(8,128)(2,1)}) %reduce-scatter.19.cloned.1.call-update) | async-done | bytes 524304
  503.2 1.3 copy.166
  504.5 0.4 copy.131
  505.0 16.5 %all_to_all.119 = bf16[128,16,128]{2,1,0:T(8,128)(2,1)S(1)} all-to-all(bf16[128,16,128]{2,1,0:T(8,128)(2,1)S(1)} %copy.131), channel_id=1, replica_groups=mesh['freq'=8,'src'=16] {'freq'}, dimensions={0} | all-to-all | bytes 1048576 | tf_op jit(solution)/shard_map/all_to_all | solution.py:55
  521.9 2.6 fusion.28
  524.6 1.1 copy.134
  525.6 1.2 copy.135
  526.8 3.5 all-to-all-start.7
  530.3 1.1 bitcast_convert_fusion.4
  531.4 8.6 %all-to-all-done.7 = bf16[16,128,128]{2,0,1:T(8,128)(2,1)S(1)} async-done(((bf16[16,128,128]{2,0,1:T(8,128)(2,1)}), bf16[16,128,128]{2,0,1:T(8,128)(2,1)S(1)}, u32[]{:S(2)}, u32[]{:S(2)}) %all-to-all-start.7) | async-done | bytes 524320 | tf_op jit(solution)/shard_map/all_to_all | solution.py:59
  540.4 1.1 bitcast_add_fusion
  (50 shorter events, 5.5 us)
Async XLA Ops:
  7.2 102.5 %reduce-scatter.13.cloned.1.call-start = ((), (), s32[]{:S(2)}) async-start(), calls=%async_computation.12 | async-start | bytes 8912896
  32.4 86.4 %copy-start.2 = (s32[16,64]{1,0:T(8,128)S(1)}, s32[16,64]{1,0:T(8,128)}, u32[]{:S(2)}) copy-start(s32[16,64]{1,0:T(8,128)} %param.5) | copy-start | bytes 12292
  112.1 16.4 %all-to-all-start = ((bf16[128,16,128]{2,1,0:T(8,128)(2,1)}), bf16[128,16,128]{2,1,0:T(8,128)(2,1)S(1)}, u32[]{:S(2)}, u32[]{:S(2)}) async-start(bf16[128,16,128]{2,1,0:T(8,128)(2,1)} %copy.96), calls=%async_computation | async-start | bytes 1048576 | tf_op jit(solution)/shard_map/all_to_all | solution.py:55
  118.7 122.7 %reduce-scatter.15.cloned.1.call-start = ((), (), s32[]{:S(2)}) async-start(), calls=%async_computation.13 | async-start | bytes 8912896
  169.6 203.7 %reduce-scatter.17.cloned.1.call-start = ((), (), s32[]{:S(2)}) async-start(), calls=%async_computation.14 | async-start | bytes 8912896
  301.6 90.6 %copy-start.1 = (bf16[1,128,512]{2,1,0:T(8,128)(2,1)S(1)}, bf16[1,128,512]{2,1,0:T(8,128)(2,1)}, u32[]{:S(2)}) copy-start(bf16[1,128,512]{2,1,0:T(8,128)(2,1)} %get-tuple-element.15) | copy-start | bytes 393220
  301.6 201.6 %reduce-scatter.19.cloned.1.call-start = ((), (), s32[]{:S(2)}) async-start(), calls=%async_computation.15 | async-start | bytes 8912896
  521.5 18.9 %copy-start = (f32[128,16,128]{2,1,0:T(8,128)S(1)}, f32[128,16,128]{2,1,0:T(8,128)}, u32[]{:S(2)}) copy-start(f32[128,16,128]{2,1,0:T(8,128)} %param.4) | copy-start | bytes 3145732
  526.8 13.2 %all-to-all-start.7 = ((bf16[16,128,128]{2,0,1:T(8,128)(2,1)}), bf16[16,128,128]{2,0,1:T(8,128)(2,1)S(1)}, u32[]{:S(2)}, u32[]{:S(2)}) async-start(bf16[16,128,128]{2,0,1:T(8,128)(2,1)} %copy.135), calls=%async_computation.7 | async-start | bytes 1048576 | tf_op jit(solution)/shard_map/all_to_all | solution.py:59
Sparse Core Ops, SparseCore 0:
  32.5 77.0 reduce-scatter.12
  169.7 71.6 reduce-scatter.14
  301.7 71.5 reduce-scatter.16
  431.7 71.4 reduce-scatter.18
where the time goes:
time: 550 us; the launch traced here: 548 us
  waiting for transfers between devices  309 us (56%)
  blocking collectives  88.1 us (16%)
  local copies, waits for them, and re-layouts  70.4 us (13%)
  matrix products  51.2 us (9%)
  between operations  14.2 us (3%)
  starting transfers between devices  10.3 us (2%)
    unnamed x8, waiting for transfers between devices  292 us
    unnamed x19, local copies, waits for them, and re-layouts  57.8 us
    all_to_all x3, blocking collectives, to_owners(): lax.all_to_all(summed, 'freq', split_axis=0, concat_axis=1, tiled=True)  49.6 us
    dot_general x4, matrix products, to_owners(): jnp.einsum('pfrs,psfk->rfk', reflection, operand, preferred_element_type=...  44 us
    all_to_all x3, blocking collectives, to_groups(): lax.all_to_all(spectrum.astype(jnp.bfloat16), 'freq', split_axis=1, conca...  38.5 us
  transfers between devices with their start and end apart: 6, of which 6 were waited for; matrix products, arithmetic and copies ran while one was open for 1% of the time, Pallas kernels for 0%

commit v1 on v0

--- a/solution.py
+++ b/solution.py
@@ -52,7 +52,10 @@
         scatter_dimension=0,
         tiled=True,
     )
-    return lax.all_to_all(summed, "freq", split_axis=0, concat_axis=1, tiled=True)
+    return jnp.concatenate(
+        lax.all_to_all(jnp.stack(jnp.split(summed, lax.axis_size("freq"), axis=0)), "freq", 0, 0),
+        axis=1,
+    )
 
 
 def to_groups(spectrum):

time: 550 us -> 589 us (1.071)
  local copies, waits for them, and re-layouts: 70.4 us -> 108 us
    another operation x0 -> x44, local copies, waits for them, and re-layouts: none -> 36.5 us  [the longest x40 34.9 us: to_owners(): jnp.stack(jnp.split(summed, lax.axis_size('freq'), axis=0))]
    unnamed x19 -> x45, local copies, waits for them, and re-layouts: 57.8 us -> 62.8 us
where the time goes in v1:
time: 589 us; the launch traced here: 587 us
  waiting for transfers between devices  308 us (52%)
  local copies, waits for them, and re-layouts  108 us (18%)
  blocking collectives  88 us (15%)
  matrix products  52.1 us (9%)
  between operations  14.4 us (2%)
  starting transfers between devices  10.5 us (2%)
  other arithmetic  6.25 us (1%)
    unnamed x8, waiting for transfers between devices  292 us
    unnamed x45, local copies, waits for them, and re-layouts  62.8 us
    all_to_all x3, blocking collectives, to_owners(): lax.all_to_all(jnp.stack(jnp.split(summed, lax.axis_size('freq'), axis=0)...  49.5 us
    dot_general x4, matrix products, to_owners(): jnp.einsum('pfrs,psfk->rfk', reflection, operand, preferred_element_type=...  44 us
    all_to_all x3, blocking collectives, to_groups(): lax.all_to_all(spectrum.astype(jnp.bfloat16), 'freq', split_axis=1, conca...  38.5 us
    another operation x40, local copies, waits for them, and re-layouts, to_owners(): jnp.stack(jnp.split(summed, lax.axis_size('freq'), axis=0))  34.9 us
  transfers between devices with their start and end apart: 6, of which 6 were waited for; matrix products, arithmetic and copies ran while one was open for 1% of the time, Pallas kernels for 0%

profile of v1, /device:TPU:0, one launch (start us, length us, event | category | flops | bytes accessed | tf_op | source)
XLA Modules:
  0.0 586.6 jit_solution(355744042234223433)
XLA Ops:
  7.2 1.6 copy.182
  9.1 11.0 %bitcast_convert_fusion.3 = bf16[16,128,2048]{2,1,0:T(8,128)(2,1)} fusion(bf16[2,16,2048,128]{3,2,1,0:T(8,128)(2,1)} %param.3, bf16[1,128,16,128]{1,3,0,2:T(8,128)(2,1)S(1)} %maximum_bitcast_fusion, bf16[1,128,16,128]{1,3,0,2:T(8,128)(2,1)S(1)} %convert_bitcast_fusion.2), kind=kOutput, calls=%fused_computation.3 | convolution fusion | flops 2152202240 | bytes 26214400 | tf_op jit(solution)/shard_map/pfrs,psfk->rfk/dot_general | solution.py:48
  20.1 12.4 %copy.240 = bf16[2048,2048]{1,0:T(8,128)(2,1)} copy(bf16[2048,2048]{0,1:T(8,128)(2,1)} %bitcast.233) | data formatting | bytes 16777216
  33.0 76.7 %reduce-scatter.13.cloned.1.call-done = bf16[128,2048]{1,0:T(8,128)(2,1)} async-done(((bf16[2048,2048]{1,0:T(8,128)(2,1)}), bf16[128,2048]{1,0:T(8,128)(2,1)}) %reduce-scatter.13.cloned.1.call-update) | async-done | bytes 524304
  109.7 1.3 copy.241
  111.0 2.7 slice_bitcast_fusion.24
  114.9 1.2 copy.155
  116.2 1.2 copy.154
  118.6 1.2 copy.152
  125.6 6.6 %all-to-all-start = ((bf16[8,16,16,128]{3,2,1,0:T(8,128)(2,1)}), bf16[8,16,16,128]{3,2,1,0:T(8,128)(2,1)S(1)}, u32[]{:S(2)}, u32[]{:S(2)}) async-start(bf16[8,16,16,128]{3,2,1,0:T(8,128)(2,1)} %constant_dynamic-update-slice_fusion), calls=%async_computation | async-start | bytes 1048576 | tf_op jit(solution)/shard_map/all_to_all | solution.py:56
  132.3 2.5 fusion.69
  134.8 7.2 %all-to-all-done = bf16[8,16,16,128]{3,2,1,0:T(8,128)(2,1)S(1)} async-done(((bf16[8,16,16,128]{3,2,1,0:T(8,128)(2,1)}), bf16[8,16,16,128]{3,2,1,0:T(8,128)(2,1)S(1)}, u32[]{:S(2)}, u32[]{:S(2)}) %all-to-all-start) | async-done | bytes 524320 | tf_op jit(solution)/shard_map/all_to_all | solution.py:56
  142.5 1.8 fusion.25
  144.8 13.1 %all_to_all.74 = bf16[16,128,128]{2,0,1:T(8,128)(2,1)S(1)} all-to-all(bf16[16,128,128]{2,0,1:T(8,128)(2,1)S(1)} %copy.160), channel_id=1, replica_groups=mesh['freq'=8,'src'=16] {'freq'}, dimensions={1} | all-to-all | bytes 1048576 | tf_op jit(solution)/shard_map/all_to_all | solution.py:62
  159.8 11.0 %bitcast_convert_fusion.2 = bf16[16,128,2048]{2,1,0:T(8,128)(2,1)} fusion(bf16[2,16,2048,128]{3,2,1,0:T(8,128)(2,1)} %param.3, bf16[1,128,16,128]{1,3,0,2:T(8,128)(2,1)S(1)} %maximum_negate_fusion, bf16[1,128,16,128]{1,3,0,2:T(8,128)(2,1)S(1)} %copy.166), kind=kOutput, calls=%fused_computation.2 | convolution fusion | flops 2152202240 | bytes 26214400 | tf_op jit(solution)/shard_map/pfrs,psfk->rfk/dot_general | solution.py:48
  170.8 12.4 %copy.242 = bf16[2048,2048]{1,0:T(8,128)(2,1)} copy(bf16[2048,2048]{0,1:T(8,128)(2,1)} %bitcast.234) | data formatting | bytes 16777216
  183.2 71.8 %reduce-scatter.15.cloned.1.call-done = bf16[128,2048]{1,0:T(8,128)(2,1)} async-done(((bf16[2048,2048]{1,0:T(8,128)(2,1)}), bf16[128,2048]{1,0:T(8,128)(2,1)}) %reduce-scatter.15.cloned.1.call-update) | async-done | bytes 524304
  255.0 1.3 copy.243
  256.3 2.7 slice_bitcast_fusion.16
  260.2 1.2 copy.174
  261.4 1.2 copy.173
  262.7 1.2 copy.172
  263.9 1.2 copy.171
  265.9 16.5 %all_to_all.75 = bf16[8,16,16,128]{3,2,1,0:T(8,128)(2,1)S(1)} all-to-all(bf16[8,16,16,128]{3,2,1,0:T(8,128)(2,1)S(1)} %constant_dynamic-update-slice_fusion.8), channel_id=1, replica_groups=mesh['freq'=8,'src'=16] {'freq'}, dimensions={0} | all-to-all | bytes 1048576 | tf_op jit(solution)/shard_map/all_to_all | solution.py:56
  282.9 1.8 fusion.26
  285.2 12.7 %all_to_all.76 = bf16[16,128,128]{2,0,1:T(8,128)(2,1)S(1)} all-to-all(bf16[16,128,128]{2,0,1:T(8,128)(2,1)S(1)} %copy.179), channel_id=1, replica_groups=mesh['freq'=8,'src'=16] {'freq'}, dimensions={1} | all-to-all | bytes 1048576 | tf_op jit(solution)/shard_map/all_to_all | solution.py:62
  299.3 1.6 copy.183
  301.1 11.0 %bitcast_convert_fusion.1 = bf16[16,128,2048]{2,1,0:T(8,128)(2,1)} fusion(bf16[2,16,2048,128]{3,2,1,0:T(8,128)(2,1)} %param.3, bf16[1,128,16,128]{1,3,0,2:T(8,128)(2,1)S(1)} %maximum_bitcast_fusion.1, bf16[1,128,16,128]{1,3,0,2:T(8,128)(2,1)S(1)} %bitcast.245), kind=kOutput, calls=%fused_computation.1 | convolution fusion | flops 2152202240 | bytes 26214400 | tf_op jit(solution)/shard_map/pfrs,psfk->rfk/dot_general | solution.py:48
  312.1 12.4 %copy.244 = bf16[2048,2048]{1,0:T(8,128)(2,1)} copy(bf16[2048,2048]{0,1:T(8,128)(2,1)} %bitcast.235) | data formatting | bytes 16777216
  324.8 71.5 %reduce-scatter.17.cloned.1.call-done = bf16[128,2048]{1,0:T(8,128)(2,1)} async-done(((bf16[2048,2048]{1,0:T(8,128)(2,1)}), bf16[128,2048]{1,0:T(8,128)(2,1)}) %reduce-scatter.17.cloned.1.call-update) | async-done | bytes 524304
  396.3 1.3 copy.245
  397.6 2.3 slice_bitcast_fusion.8
  401.1 1.2 copy.192
  402.4 1.2 copy.191
  404.8 16.5 %all_to_all.77 = bf16[8,16,16,128]{3,2,1,0:T(8,128)(2,1)S(1)} all-to-all(bf16[8,16,16,128]{3,2,1,0:T(8,128)(2,1)S(1)} %constant_dynamic-update-slice_fusion.16), channel_id=1, replica_groups=mesh['freq'=8,'src'=16] {'freq'}, dimensions={0} | all-to-all | bytes 1048576 | tf_op jit(solution)/shard_map/all_to_all | solution.py:56
  421.8 1.8 fusion.27
  424.1 12.7 %all_to_all.78 = bf16[16,128,128]{2,0,1:T(8,128)(2,1)S(1)} all-to-all(bf16[16,128,128]{2,0,1:T(8,128)(2,1)S(1)} %copy.197), channel_id=1, replica_groups=mesh['freq'=8,'src'=16] {'freq'}, dimensions={1} | all-to-all | bytes 1048576 | tf_op jit(solution)/shard_map/all_to_all | solution.py:62
  438.8 11.0 %bitcast_convert_fusion = bf16[16,128,2048]{2,1,0:T(8,128)(2,1)} fusion(bf16[2,16,2048,128]{3,2,1,0:T(8,128)(2,1)} %param.3, bf16[1,128,16,128]{1,3,0,2:T(8,128)(2,1)S(1)} %maximum_negate_fusion.1, bf16[1,128,16,128]{1,3,0,2:T(8,128)(2,1)S(1)} %copy.203), kind=kOutput, calls=%fused_computation | convolution fusion | flops 2152202240 | bytes 26214400 | tf_op jit(solution)/shard_map/pfrs,psfk->rfk/dot_general | solution.py:48
  449.8 12.4 %copy.246 = bf16[2048,2048]{1,0:T(8,128)(2,1)} copy(bf16[2048,2048]{0,1:T(8,128)(2,1)} %bitcast.236) | data formatting | bytes 16777216
  462.2 71.6 %reduce-scatter.19.cloned.1.call-done = bf16[128,2048]{1,0:T(8,128)(2,1)} async-done(((bf16[2048,2048]{1,0:T(8,128)(2,1)}), bf16[128,2048]{1,0:T(8,128)(2,1)}) %reduce-scatter.19.cloned.1.call-update) | async-done | bytes 524304
  533.8 1.3 copy.247
  535.1 2.5 slice_bitcast_fusion
  538.8 1.2 copy.211
  540.1 1.2 copy.210
  543.5 16.5 %all_to_all.79 = bf16[8,16,16,128]{3,2,1,0:T(8,128)(2,1)S(1)} all-to-all(bf16[8,16,16,128]{3,2,1,0:T(8,128)(2,1)S(1)} %constant_dynamic-update-slice_fusion.24), channel_id=1, replica_groups=mesh['freq'=8,'src'=16] {'freq'}, dimensions={0} | all-to-all | bytes 1048576 | tf_op jit(solution)/shard_map/all_to_all | solution.py:56
  560.5 2.6 fusion.28
  565.4 3.5 all-to-all-start.7
  570.0 8.6 %all-to-all-done.7 = bf16[16,128,128]{2,0,1:T(8,128)(2,1)S(1)} async-done(((bf16[16,128,128]{2,0,1:T(8,128)(2,1)}), bf16[16,128,128]{2,0,1:T(8,128)(2,1)S(1)}, u32[]{:S(2)}, u32[]{:S(2)}) %all-to-all-start.7) | async-done | bytes 524320 | tf_op jit(solution)/shard_map/all_to_all | solution.py:62
  (112 shorter events, 30.5 us)
Async XLA Ops:
  7.2 102.5 %reduce-scatter.13.cloned.1.call-start = ((), (), s32[]{:S(2)}) async-start(), calls=%async_computation.12 | async-start | bytes 8912896
  32.5 99.8 %copy-start.1 = (s32[16,64]{1,0:T(8,128)S(1)}, s32[16,64]{1,0:T(8,128)}, u32[]{:S(2)}) copy-start(s32[16,64]{1,0:T(8,128)} %param.5) | copy-start | bytes 12292
  125.6 16.4 %all-to-all-start = ((bf16[8,16,16,128]{3,2,1,0:T(8,128)(2,1)}), bf16[8,16,16,128]{3,2,1,0:T(8,128)(2,1)S(1)}, u32[]{:S(2)}, u32[]{:S(2)}) async-start(bf16[8,16,16,128]{3,2,1,0:T(8,128)(2,1)} %constant_dynamic-update-slice_fusion), calls=%async_computation | async-start | bytes 1048576 | tf_op jit(solution)/shard_map/all_to_all | solution.py:56
  132.2 122.8 %reduce-scatter.15.cloned.1.call-start = ((), (), s32[]{:S(2)}) async-start(), calls=%async_computation.13 | async-start | bytes 8912896
  183.2 213.1 %reduce-scatter.17.cloned.1.call-start = ((), (), s32[]{:S(2)}) async-start(), calls=%async_computation.14 | async-start | bytes 8912896
  324.5 209.3 %reduce-scatter.19.cloned.1.call-start = ((), (), s32[]{:S(2)}) async-start(), calls=%async_computation.15 | async-start | bytes 8912896
  560.0 18.9 %copy-start = (f32[128,16,128]{2,1,0:T(8,128)S(1)}, f32[128,16,128]{2,1,0:T(8,128)}, u32[]{:S(2)}) copy-start(f32[128,16,128]{2,1,0:T(8,128)} %param.4) | copy-start | bytes 3145732
  565.4 13.2 %all-to-all-start.7 = ((bf16[16,128,128]{2,0,1:T(8,128)(2,1)}), bf16[16,128,128]{2,0,1:T(8,128)(2,1)S(1)}, u32[]{:S(2)}, u32[]{:S(2)}) async-start(bf16[16,128,128]{2,0,1:T(8,128)(2,1)} %copy.216), calls=%async_computation.7 | async-start | bytes 1048576 | tf_op jit(solution)/shard_map/all_to_all | solution.py:62
Sparse Core Ops, SparseCore 0:
  32.6 77.0 reduce-scatter.12
  183.3 71.6 reduce-scatter.14
  324.6 71.6 reduce-scatter.16
  462.3 71.4 reduce-scatter.18
